TPU v7x, 512 devices: a whole 4x8x8 slice. The times are simulated.
512 devices in a mesh: ent: 128 (over y, z, core), rep: 4 (over x).
Axes of the slice: x: 4, y: 8, z: 8, core: 2. Of those that a mesh axis runs over, the one named last changes fastest.
Arguments:
- entity_table: float32 [65536, 200], P('ent'), may hold values from -6 to 6
- relation_table: bfloat16 [822, 200], replicated, may hold values from -12 to 12
- filters: float32 [32, 9], replicated, may hold values from -2 to 2
- projection: bfloat16 [9728, 200], replicated, may hold values from -0.0625 to 0.0625
- request_owner: int32 [163840, 1], P(('ent', 'rep')), may hold values from 0 to 127; in each aligned block of 320 rows (0 to 319, 320 to 639, ...) at most 4 rows name the same one
- request_row: int32 [163840], P(('ent', 'rep')), may hold values from 0 to 511
- relation_id: int32 [65536], P(('ent', 'rep')), may hold values from 0 to 821
- rare_flag: int32 [65536], P('ent'), may hold values 0 or 1
- running_norm: float32 [], replicated, may hold values from 2 to 6
Outputs:
- new_table: float32 [65536, 200], P('ent')
- filter_grad: float32 [32, 9], replicated
Inputs may be any that keep to these rules, and one draw needn't show every extreme that they name: `request_owner`: among the requests of one device no owner shard is named more than 4 times, a bound that some block reaches.
All inputs are finite; a program needn't handle non-finite values. No bound on the sum of `rare_flag` on one device may be relied on, other than what follows from the above.
Results may differ from a plain program's by a relative error of at most 0.002.
Values sent between devices are 32-bit elements; how exact they have to be, the bound alone decides.
A program may use at most 64 MiB of HBM per device.

v0:
```python
import jax
import jax.numpy as jnp
from jax import lax
from jax.sharding import PartitionSpec as P

D = 200
ROWS = 20
learn_rate = 0.5
norm_eps = 1e-06


def conv_act(head_rows, rel_rows, filters):
    count = head_rows.shape[0]
    stacked = jnp.concatenate(
        [head_rows.reshape(count, ROWS, D // ROWS), rel_rows.reshape(count, ROWS, D // ROWS)],
        axis=1,
    )[:, None]
    kernel = filters.reshape(filters.shape[0], 1, 3, 3)
    conv_out = lax.conv_general_dilated(
        stacked, kernel, (1, 1), "VALID", precision=lax.Precision.HIGHEST
    )
    return jax.nn.silu(conv_out).reshape(count, -1)


def block_step(row_values, rel_rows, filters, projection, batch_rows, neg_count):
    head_rows = row_values[:batch_rows]
    pos_rows = row_values[batch_rows : 2 * batch_rows]
    neg_rows = row_values[2 * batch_rows :]
    activated, pullback = jax.vjp(
        lambda head_part, filt_part: conv_act(head_part, rel_rows, filt_part), head_rows, filters
    )
    features = activated.astype(jnp.bfloat16)
    projected = jnp.dot(features, projection, preferred_element_type=jnp.float32)
    sig_proj = jax.nn.sigmoid(projected)
    hidden = projected * sig_proj
    score_pos = jnp.sum(hidden * pos_rows, 1)
    score_neg = jnp.dot(hidden, neg_rows.T, precision=lax.Precision.HIGHEST)
    grad_pos = -jax.nn.sigmoid(-score_pos)
    grad_neg = jax.nn.sigmoid(score_neg) / neg_count
    pos_grad_rows = grad_pos[:, None] * hidden
    neg_grad_rows = jnp.dot(grad_neg.T, hidden, precision=lax.Precision.HIGHEST)
    grad_hidden = grad_pos[:, None] * pos_rows + jnp.dot(
        grad_neg, neg_rows, precision=lax.Precision.HIGHEST
    )
    grad_proj = (grad_hidden * sig_proj * (1.0 + projected * (1.0 - sig_proj))).astype(jnp.bfloat16)
    grad_feat = lax.dot_general(
        grad_proj, projection, (((1,), (1,)), ((), ())), preferred_element_type=jnp.float32
    )
    head_grad_rows, filter_part = pullback(grad_feat)
    return (jnp.concatenate([head_grad_rows, pos_grad_rows, neg_grad_rows], axis=0), filter_part)


def body(
    entity_table,
    relation_table,
    filters,
    projection,
    request_owner,
    request_row,
    relation_id,
    rare_flag,
    running_norm,
):
    ent_count = lax.axis_size("ent")
    rep_count = lax.axis_size("rep")
    req_count = request_row.shape[0]
    batch_rows = relation_id.shape[0]
    neg_count = req_count - 2 * batch_rows
    width = entity_table.shape[1]
    slots_each = max(2, 3 * req_count // (2 * ent_count) + 1)
    owner_shard = request_owner[:, 0]
    onehot = (owner_shard[:, None] == jnp.arange(ent_count, dtype=jnp.int32)[None, :]).astype(
        jnp.int32
    )
    slot_index = jnp.sum(jnp.cumsum(onehot, 0) * onehot, 1) - 1
    slot_place = owner_shard * slots_each + slot_index
    send_ids = (
        jnp.zeros((ent_count * slots_each,), jnp.int32)
        .at[slot_place]
        .set(request_row)
        .reshape(ent_count, slots_each)
    )
    wanted = lax.all_to_all(send_ids, "ent", split_axis=0, concat_axis=0, tiled=True)
    found_rows = entity_table[wanted]
    fetched = lax.all_to_all(found_rows, "ent", split_axis=0, concat_axis=0, tiled=True)
    row_values = fetched.reshape(-1, width)[slot_place]
    rel_rows = relation_table[relation_id].astype(jnp.float32)
    grads, filter_part = block_step(
        row_values, rel_rows, filters, projection, batch_rows, neg_count
    )
    send_grads = (
        jnp.zeros((ent_count * slots_each, width), jnp.float32)
        .at[slot_place]
        .set(grads)
        .reshape(ent_count, slots_each, width)
    )
    received = lax.all_to_all(send_grads, "ent", split_axis=0, concat_axis=0, tiled=True)
    all_ids = lax.all_gather(wanted, "rep", axis=0, tiled=True)
    all_grads = lax.all_gather(received, "rep", axis=0, tiled=True)
    summed_grad = (
        jnp.zeros(entity_table.shape, jnp.float32)
        .at[all_ids.reshape(-1)]
        .add(all_grads.reshape(-1, width))
    )
    updated = entity_table - learn_rate * summed_grad
    row_norms = jnp.sqrt(jnp.sum(updated * updated, 1) + norm_eps)
    local_norm = jnp.sum(row_norms)
    filter_total = lax.psum(filter_part, ("ent", "rep"))
    norm_total = lax.psum(local_norm, "ent")
    filter_grad = filter_total / (batch_rows * ent_count * rep_count)
    target = 0.25 * running_norm + 0.75 * norm_total / (entity_table.shape[0] * ent_count)
    new_table = jnp.where(
        (rare_flag == 1)[:, None], updated * (target / row_norms)[:, None], updated
    )
    return (new_table, filter_grad)


def solution(mesh):
    in_specs = (
        P("ent", None),
        P(),
        P(),
        P(),
        P(("ent", "rep"), None),
        P(("ent", "rep")),
        P(("ent", "rep")),
        P("ent"),
        P(),
    )
    out_specs = (P("ent", None), P())
    return jax.shard_map(body, mesh=mesh, in_specs=in_specs, out_specs=out_specs, check_vma=False)
```

profile of v0, /device:TPU:1, one launch (start us, length us, event | category | flops | bytes accessed | tf_op | source)
XLA Modules:
  0.0 538.2 jit_solution(8350565503353187962)
XLA Ops:
  7.2 0.7 reduce
  8.3 0.2 fusion.15
  8.5 0.7 fusion.22
  9.2 3.1 scatter_custom_fusion
  12.3 0.7 all_to_all.16
  13.1 18.4 %all-to-all-start = ((s32[128,1,4]{2,1,0:T(1,128)}), s32[128,1,4]{2,1,0:T(1,128)S(1)}, u32[]{:S(2)}, u32[]{:S(2)}) async-start(s32[128,1,4]{2,1,0:T(1,128)} %bitcast.4), calls=%async_computation | async-start | bytes 131072 | tf_op jit(solution)/shard_map/all_to_all | solution.py:83
  31.5 1.2 copy.117
  32.7 10.2 %all-to-all-done = s32[128,1,4]{2,1,0:T(1,128)S(1)} async-done(((s32[128,1,4]{2,1,0:T(1,128)}), s32[128,1,4]{2,1,0:T(1,128)S(1)}, u32[]{:S(2)}, u32[]{:S(2)}) %all-to-all-start) | async-done | bytes 2080 | tf_op jit(solution)/shard_map/all_to_all | solution.py:83
  43.1 0.5 copy-done.2
  43.6 1.6 gather_fusion
  45.1 0.9 reshape.144
  46.1 5.7 %all-to-all-start.1 = ((f32[128,4,200]{2,1,0:T(4,128)}), f32[128,4,200]{2,1,0:T(4,128)S(1)}, u32[]{:S(2)}, u32[]{:S(2)}) async-start(f32[128,4,200]{2,1,0:T(4,128)} %reshape.144), calls=%async_computation.1 | async-start | bytes 1048576 | tf_op jit(solution)/shard_map/all_to_all | solution.py:85
  51.8 0.5 all-gather.3.cloned.1.call-start
  52.3 0.2 copy.100
  52.6 0.8 gather_fusion.2
  53.6 17.8 %all-to-all-done.1 = f32[128,4,200]{2,1,0:T(4,128)S(1)} async-done(((f32[128,4,200]{2,1,0:T(4,128)}), f32[128,4,200]{2,1,0:T(4,128)S(1)}, u32[]{:S(2)}, u32[]{:S(2)}) %all-to-all-start.1) | async-done | bytes 409632 | tf_op jit(solution)/shard_map/all_to_all | solution.py:85
  71.4 0.2 reshape.133
  71.6 1.6 gather_fusion.1
  73.2 0.7 fusion.28
  74.1 7.1 %multiply_convert_fusion = (bf16[128,32,38,8]{0,1,3,2:T(8,128)(2,1)S(1)}, f32[128,32,38,8]{0,1,3,2:T(8,128)}) fusion(f32[32,1,3,3]{0,1,3,2:T(1,128)S(1)} %reshape.195, f32[128,1,40,10]{0,2,3,1:T(8,128)S(1)} %bitcast.46), kind=kOutput, calls=%fused_computation.9 | convolution fusion | flops 140705792 | bytes 7677056 | tf_op jit(solution)/shard_map/jvp()/conv_general_dilated | solution.py:19
  81.2 1.0 copy.105
  82.1 1.6 copy.123
  83.8 3.5 multiply_reduce_fusion.1
  87.2 0.3 fusion.8
  87.6 0.3 fusion.25
  87.9 0.4 fusion.4
  88.3 2.0 fusion.30
  90.4 2.6 fusion.1
  93.1 2.2 copy-done
  95.3 23.1 %fusion.29 = f32[128,1,40,10]{0,1,3,2:T(1,128)S(1)} fusion(f32[128,32,38,8]{0,1,3,2:T(8,128)S(1)} %fusion.1, f32[32,1,3,3]{0,1,3,2:T(1,128)S(1)} %reshape.195), kind=kOutput, calls=%fused_computation.68 | convolution fusion | flops 134479872 | bytes 5186688 | tf_op jit(solution)/shard_map/transpose(jvp())/conv_general_dilated | solution.py:19
  118.5 0.1 copy.114
  118.7 1.9 scatter_custom_fusion.1
  120.6 0.2 reshape.138
  120.7 26.3 %all_to_all.25 = f32[128,4,200]{2,1,0:T(4,128)S(1)} all-to-all(f32[128,4,200]{2,1,0:T(4,128)S(1)} %reshape.138), channel_id=1, replica_groups=mesh['ent'=128,'rep'=4] {'ent'}, dimensions={0} | all-to-all | bytes 819200 | tf_op jit(solution)/shard_map/all_to_all | solution.py:97
  147.0 1.0 copy.115
  148.7 8.4 %all-gather = s32[512,1,4]{0,2,1:T(4,128)S(1)} all-gather(s32[128,1,4]{0,2,1:T(4,128)S(1)} %copy.96), channel_id=2, replica_groups=mesh['ent'=128,'rep'=4] {'rep'}, dimensions={0}, use_global_device_ids=true | all-gather | bytes 10240 | tf_op jit(solution)/shard_map/all_gather | solution.py:98
  157.3 0.2 reshape.132
  157.5 9.4 %convolution_reduce_fusion = f32[32,3,3]{0,2,1:T(4,128)S(1)} fusion(f32[128,32,38,8]{0,1,3,2:T(8,128)} %copy-done, f32[128,1,40,10]{0,2,3,1:T(8,128)S(1)} %bitcast.47), kind=kOutput, calls=%fused_computation.20 | convolution fusion | flops 134479872 | bytes 5186688 | tf_op jit(solution)/shard_map/transpose(jvp())/conv_general_dilated | solution.py:19
  166.9 97.7 %psum.15 = f32[32,9]{0,1:T(8,128)S(1)} all-reduce(f32[32,9]{0,1:T(8,128)S(1)} %reshape.140), channel_id=1, replica_groups=mesh['ent'=128,'rep'=4] {'ent','rep'}, use_global_device_ids=true, to_apply=%region_10.11 | all-reduce | flops 288 | bytes 2304 | tf_op jit(solution)/shard_map/psum | solution.py:108
  264.6 2.0 copy.116
  266.6 1.8 reshape.187
  268.3 12.1 %scatter_custom_fusion.2 = f32[512,200]{1,0:T(8,128)S(1)} fusion(s32[2048]{0:T(1024)S(1)} %bitcast.53, f32[2048,200]{1,0:T(8,128)} %reshape.187, f32[]{:T(128)} %constant.16.clone.1), kind=kCustom, calls=%fused_computation.28 | custom fusion | flops 409600 | bytes 410112 | tf_op jit(solution)/shard_map/scatter-add | solution.py:103
  280.4 0.2 multiply_reduce_fusion
  280.6 0.6 sqrt_reduce_fusion
  281.2 0.6 broadcast_multiply_fusion.1
  281.8 247.5 %psum.14 = f32[]{:T(128)} all-reduce(f32[]{:T(128)} %sqrt_reduce_fusion), channel_id=1, replica_groups=mesh['ent'=128,'rep'=4] {'ent'}, use_global_device_ids=true, to_apply=%region_9.10 | all-reduce | flops 1 | bytes 8 | tf_op jit(solution)/shard_map/psum | solution.py:109
  529.9 0.2 multiply_select_fusion
  530.1 0.9 copy.119
  (59 shorter events, 1.3 us)
Async XLA Ops:
  8.0 44.3 %copy-start.5 = (bf16[822,200]{0,1:T(8,128)(2,1)S(1)}, bf16[822,200]{0,1:T(8,128)(2,1)}, u32[]{:S(2)}) copy-start(bf16[822,200]{0,1:T(8,128)(2,1)} %param.10) | copy-start | bytes 986404
  8.2 44.3 %copy-start.9 = (s32[128]{0:T(128)S(1)}, s32[128]{0:T(128)}, u32[]{:S(2)}) copy-start(s32[128]{0:T(128)} %param.15) | copy-start | bytes 1540
  8.5 45.1 %copy-start.6 = (f32[32,9]{0,1:T(8,128)S(1)}, f32[32,9]{0,1:T(8,128)}, u32[]{:S(2)}) copy-start(f32[32,9]{0,1:T(8,128)} %param.11) | copy-start | bytes 3460
  9.2 62.3 %copy-start.7 = (s32[320]{0:T(512)}, s32[320]{0:T(512)S(1)}, u32[]{:S(2)}) copy-start(s32[320]{0:T(512)S(1)} %fusion.22) | copy-start | bytes 3844
  13.1 29.9 %all-to-all-start = ((s32[128,1,4]{2,1,0:T(1,128)}), s32[128,1,4]{2,1,0:T(1,128)S(1)}, u32[]{:S(2)}, u32[]{:S(2)}) async-start(s32[128,1,4]{2,1,0:T(1,128)} %bitcast.4), calls=%async_computation | async-start | bytes 131072 | tf_op jit(solution)/shard_map/all_to_all | solution.py:83
  42.9 0.6 copy-start.2
  46.1 25.3 %all-to-all-start.1 = ((f32[128,4,200]{2,1,0:T(4,128)}), f32[128,4,200]{2,1,0:T(4,128)S(1)}, u32[]{:S(2)}, u32[]{:S(2)}) async-start(f32[128,4,200]{2,1,0:T(4,128)} %reshape.144), calls=%async_computation.1 | async-start | bytes 1048576 | tf_op jit(solution)/shard_map/all_to_all | solution.py:85
  51.8 212.8 %all-gather.3.cloned.1.call-start = ((), (), s32[]{:S(2)}) async-start(), calls=%async_computation.3 | async-start | bytes 2048000 | tf_op jit(solution)/shard_map/all_gather | solution.py:99
  83.8 4.1 copy-start.4
  83.8 4.5 copy-start.1
  87.5 2.8 slice-start
  88.3 2.1 slice-start.1
  93.1 2.2 copy-start
  95.3 53.4 %copy-start.8 = (s32[512]{0:T(512)S(1)}, s32[512]{0:T(512)}, u32[]{:S(2)}) copy-start(s32[512]{0:T(512)} %param.16) | copy-start | bytes 6148
  95.3 53.4 %copy-start.3 = (s32[128,1,4]{2,1,0:T(1,128)S(1)}, s32[128,1,4]{2,1,0:T(1,128)}, u32[]{:S(2)}) copy-start(s32[128,1,4]{2,1,0:T(1,128)} %copy-done.2) | copy-start | bytes 6148
Sparse Core Ops, SparseCore 0:
  148.1 28.8 all-gather.2
where the time goes:
time: 544 us; the launch traced here: 538 us
  blocking collectives  380 us (70%)
  matrix products  46 us (8%)
  waiting for transfers between devices  28 us (5%)
  local copies, waits for them, and re-layouts  25.1 us (5%)
  starting transfers between devices  24.6 us (5%)
  other arithmetic  18.4 us (3%)
  between operations  16.1 us (3%)
    psum x1, blocking collectives, body(): norm_total = lax.psum(local_norm, 'ent')  247 us
    psum x1, blocking collectives, body(): filter_total = lax.psum(filter_part, ('ent', 'rep'))  97.7 us
    conv_general_dilated x3, matrix products, conv_act(): lax.conv_general_dilated(stacked, kernel, (1, 1), 'VALID', precision=lax....  39.5 us
    all_to_all x1, blocking collectives, body(): lax.all_to_all(send_grads, 'ent', split_axis=0, concat_axis=0, tiled=True)  26.3 us
    all_to_all x1, starting transfers between devices, body(): lax.all_to_all(send_ids, 'ent', split_axis=0, concat_axis=0, tiled=True)  18.4 us
    all_to_all x1, waiting for transfers between devices, body(): lax.all_to_all(found_rows, 'ent', split_axis=0, concat_axis=0, tiled=True)  17.8 us
    scatter-add x1, other arithmetic, body(): summed_grad = jnp.zeros(entity_table.shape, jnp.float32).at[all_ids.resha...  12.1 us
  transfers between devices with their start and end apart: 3, of which 2 were waited for; matrix products, arithmetic and copies ran while one was open for 2% of the time, Pallas kernels for 0%

commit v1 on v0

--- a/solution.py
+++ b/solution.py
@@ -105,7 +105,8 @@
     updated = entity_table - learn_rate * summed_grad
     row_norms = jnp.sqrt(jnp.sum(updated * updated, 1) + norm_eps)
     local_norm = jnp.sum(row_norms)
-    filter_total = lax.psum(filter_part, ("ent", "rep"))
+    half = lax.psum(filter_part, "rep")
+    filter_total = lax.psum(half, "ent")
     norm_total = lax.psum(local_norm, "ent")
     filter_grad = filter_total / (batch_rows * ent_count * rep_count)
     target = 0.25 * running_norm + 0.75 * norm_total / (entity_table.shape[0] * ent_count)

time: 544 us -> 469 us (0.86)
  blocking collectives: 380 us -> 302 us
    psum x1, blocking collectives: 97.7 us -> 8.32 us  [body(): half = lax.psum(filter_part, 'rep')]
    psum x1, blocking collectives: 247 us -> 259 us  [body(): norm_total = lax.psum(local_norm, 'ent')]
  transfers between devices with their start and end apart: 3 -> 3, of which waited for: 2 -> 3; matrix products, arithmetic and copies ran while one was open for 2% -> 3% of each run, Pallas kernels for 0% -> 0%
where the time goes in v1:
time: 469 us; the launch traced here: 462 us
  blocking collectives  302 us (64%)
  matrix products  46 us (10%)
  waiting for transfers between devices  29.8 us (6%)
  local copies, waits for them, and re-layouts  25.1 us (5%)
  starting transfers between devices  24.6 us (5%)
  other arithmetic  18.4 us (4%)
  between operations  16.1 us (3%)
    psum x1, blocking collectives, body(): norm_total = lax.psum(local_norm, 'ent')  259 us
    conv_general_dilated x3, matrix products, conv_act(): lax.conv_general_dilated(stacked, kernel, (1, 1), 'VALID', precision=lax....  39.5 us
    all_to_all x1, blocking collectives, body(): lax.all_to_all(send_grads, 'ent', split_axis=0, concat_axis=0, tiled=True)  26.3 us
    all_to_all x1, starting transfers between devices, body(): lax.all_to_all(send_ids, 'ent', split_axis=0, concat_axis=0, tiled=True)  18.4 us
    all_to_all x1, waiting for transfers between devices, body(): lax.all_to_all(found_rows, 'ent', split_axis=0, concat_axis=0, tiled=True)  17.8 us
    scatter-add x1, other arithmetic, body(): summed_grad = jnp.zeros(entity_table.shape, jnp.float32).at[all_ids.resha...  12.1 us
    all_to_all x1, waiting for transfers between devices, body(): lax.all_to_all(send_ids, 'ent', split_axis=0, concat_axis=0, tiled=True)  10.2 us
  transfers between devices with their start and end apart: 3, of which 3 were waited for; matrix products, arithmetic and copies ran while one was open for 3% of the time, Pallas kernels for 0%

profile of v1, /device:TPU:1, one launch (start us, length us, event | category | flops | bytes accessed | tf_op | source)
XLA Modules:
  0.0 461.9 jit_solution(11373424271101292609)
XLA Ops:
  7.2 0.7 reduce
  8.3 0.2 fusion.15
  8.5 0.7 fusion.22
  9.2 3.1 scatter_custom_fusion
  12.3 0.7 all_to_all.16
  13.1 18.4 %all-to-all-start = ((s32[128,1,4]{2,1,0:T(1,128)}), s32[128,1,4]{2,1,0:T(1,128)S(1)}, u32[]{:S(2)}, u32[]{:S(2)}) async-start(s32[128,1,4]{2,1,0:T(1,128)} %bitcast.4), calls=%async_computation | async-start | bytes 131072 | tf_op jit(solution)/shard_map/all_to_all | solution.py:83
  31.5 1.2 copy.117
  32.7 10.2 %all-to-all-done = s32[128,1,4]{2,1,0:T(1,128)S(1)} async-done(((s32[128,1,4]{2,1,0:T(1,128)}), s32[128,1,4]{2,1,0:T(1,128)S(1)}, u32[]{:S(2)}, u32[]{:S(2)}) %all-to-all-start) | async-done | bytes 2080 | tf_op jit(solution)/shard_map/all_to_all | solution.py:83
  43.1 0.5 copy-done.2
  43.6 1.6 gather_fusion
  45.1 0.9 reshape.144
  46.1 5.7 %all-to-all-start.1 = ((f32[128,4,200]{2,1,0:T(4,128)}), f32[128,4,200]{2,1,0:T(4,128)S(1)}, u32[]{:S(2)}, u32[]{:S(2)}) async-start(f32[128,4,200]{2,1,0:T(4,128)} %reshape.144), calls=%async_computation.1 | async-start | bytes 1048576 | tf_op jit(solution)/shard_map/all_to_all | solution.py:85
  51.8 0.5 all-gather.3.cloned.1.call-start
  52.3 0.2 copy.100
  52.6 0.8 gather_fusion.2
  53.6 17.8 %all-to-all-done.1 = f32[128,4,200]{2,1,0:T(4,128)S(1)} async-done(((f32[128,4,200]{2,1,0:T(4,128)}), f32[128,4,200]{2,1,0:T(4,128)S(1)}, u32[]{:S(2)}, u32[]{:S(2)}) %all-to-all-start.1) | async-done | bytes 409632 | tf_op jit(solution)/shard_map/all_to_all | solution.py:85
  71.4 0.2 reshape.133
  71.6 1.6 gather_fusion.1
  73.2 0.7 fusion.28
  74.1 7.1 %multiply_convert_fusion = (bf16[128,32,38,8]{0,1,3,2:T(8,128)(2,1)S(1)}, f32[128,32,38,8]{0,1,3,2:T(8,128)}) fusion(f32[32,1,3,3]{0,1,3,2:T(1,128)S(1)} %reshape.195, f32[128,1,40,10]{0,2,3,1:T(8,128)S(1)} %bitcast.46), kind=kOutput, calls=%fused_computation.9 | convolution fusion | flops 140705792 | bytes 7677056 | tf_op jit(solution)/shard_map/jvp()/conv_general_dilated | solution.py:19
  81.2 1.0 copy.105
  82.1 1.6 copy.123
  83.8 3.5 multiply_reduce_fusion.1
  87.2 0.3 fusion.8
  87.6 0.3 fusion.25
  87.9 0.4 fusion.4
  88.3 2.0 fusion.30
  90.4 2.6 fusion.1
  93.1 2.2 copy-done
  95.3 23.1 %fusion.29 = f32[128,1,40,10]{0,1,3,2:T(1,128)S(1)} fusion(f32[128,32,38,8]{0,1,3,2:T(8,128)S(1)} %fusion.1, f32[32,1,3,3]{0,1,3,2:T(1,128)S(1)} %reshape.195), kind=kOutput, calls=%fused_computation.68 | convolution fusion | flops 134479872 | bytes 5186688 | tf_op jit(solution)/shard_map/transpose(jvp())/conv_general_dilated | solution.py:19
  118.7 1.9 scatter_custom_fusion.1
  120.6 0.2 reshape.138
  120.7 26.3 %all_to_all.25 = f32[128,4,200]{2,1,0:T(4,128)S(1)} all-to-all(f32[128,4,200]{2,1,0:T(4,128)S(1)} %reshape.138), channel_id=1, replica_groups=mesh['ent'=128,'rep'=4] {'ent'}, dimensions={0} | all-to-all | bytes 819200 | tf_op jit(solution)/shard_map/all_to_all | solution.py:97
  147.0 1.0 copy.115
  148.7 8.4 %all-gather = s32[512,1,4]{0,2,1:T(4,128)S(1)} all-gather(s32[128,1,4]{0,2,1:T(4,128)S(1)} %copy.96), channel_id=2, replica_groups=mesh['ent'=128,'rep'=4] {'rep'}, dimensions={0}, use_global_device_ids=true | all-gather | bytes 10240 | tf_op jit(solution)/shard_map/all_gather | solution.py:98
  157.3 0.2 reshape.132
  157.5 9.4 %convolution_reduce_fusion = f32[32,3,3]{0,2,1:T(4,128)S(1)} fusion(f32[128,32,38,8]{0,1,3,2:T(8,128)} %copy-done, f32[128,1,40,10]{0,2,3,1:T(8,128)S(1)} %bitcast.47), kind=kOutput, calls=%fused_computation.20 | convolution fusion | flops 134479872 | bytes 5186688 | tf_op jit(solution)/shard_map/transpose(jvp())/conv_general_dilated | solution.py:19
  166.9 8.3 %psum.22 = f32[32,9]{0,1:T(8,128)S(1)} all-reduce(f32[32,9]{0,1:T(8,128)S(1)} %reshape.140), channel_id=1, replica_groups=mesh['ent'=128,'rep'=4] {'rep'}, use_global_device_ids=true, to_apply=%region_10.11 | all-reduce | flops 288 | bytes 2304 | tf_op jit(solution)/shard_map/psum | solution.py:108
  175.2 1.8 all-gather.3.cloned.1.call-done
  177.0 2.0 copy.116
  179.0 1.8 reshape.187
  180.7 12.1 %scatter_custom_fusion.2 = f32[512,200]{1,0:T(8,128)S(1)} fusion(s32[2048]{0:T(1024)S(1)} %bitcast.53, f32[2048,200]{1,0:T(8,128)} %reshape.187, f32[]{:T(128)} %constant.16.clone.1), kind=kCustom, calls=%fused_computation.28 | custom fusion | flops 409600 | bytes 410112 | tf_op jit(solution)/shard_map/scatter-add | solution.py:103
  192.8 0.2 multiply_reduce_fusion
  193.0 0.6 sqrt_reduce_fusion
  193.6 258.8 %all-reduce.1 = (f32[]{:T(128)}, f32[32,9]{0,1:T(8,128)S(1)}) all-reduce(f32[]{:T(128)} %sqrt_reduce_fusion, f32[32,9]{0,1:T(8,128)S(1)} %psum.22), channel_id=1, replica_groups=mesh['ent'=128,'rep'=4] {'ent'}, use_global_device_ids=true, to_apply=%region_9.10 | all-reduce | flops 289 | bytes 2312 | tf_op jit(solution)/shard_map/psum | solution.py:110
  453.1 0.2 multiply_select_fusion
  453.3 0.9 copy.119
  454.3 0.6 broadcast_multiply_fusion.1
  (59 shorter events, 1.4 us)
Async XLA Ops:
  8.0 44.3 %copy-start.5 = (bf16[822,200]{0,1:T(8,128)(2,1)S(1)}, bf16[822,200]{0,1:T(8,128)(2,1)}, u32[]{:S(2)}) copy-start(bf16[822,200]{0,1:T(8,128)(2,1)} %param.10) | copy-start | bytes 986404
  8.2 44.3 %copy-start.9 = (s32[128]{0:T(128)S(1)}, s32[128]{0:T(128)}, u32[]{:S(2)}) copy-start(s32[128]{0:T(128)} %param.15) | copy-start | bytes 1540
  8.5 45.1 %copy-start.6 = (f32[32,9]{0,1:T(8,128)S(1)}, f32[32,9]{0,1:T(8,128)}, u32[]{:S(2)}) copy-start(f32[32,9]{0,1:T(8,128)} %param.11) | copy-start | bytes 3460
  9.2 62.3 %copy-start.7 = (s32[320]{0:T(512)}, s32[320]{0:T(512)S(1)}, u32[]{:S(2)}) copy-start(s32[320]{0:T(512)S(1)} %fusion.22) | copy-start | bytes 3844
  13.1 29.9 %all-to-all-start = ((s32[128,1,4]{2,1,0:T(1,128)}), s32[128,1,4]{2,1,0:T(1,128)S(1)}, u32[]{:S(2)}, u32[]{:S(2)}) async-start(s32[128,1,4]{2,1,0:T(1,128)} %bitcast.4), calls=%async_computation | async-start | bytes 131072 | tf_op jit(solution)/shard_map/all_to_all | solution.py:83
  42.9 0.6 copy-start.2
  46.1 25.3 %all-to-all-start.1 = ((f32[128,4,200]{2,1,0:T(4,128)}), f32[128,4,200]{2,1,0:T(4,128)S(1)}, u32[]{:S(2)}, u32[]{:S(2)}) async-start(f32[128,4,200]{2,1,0:T(4,128)} %reshape.144), calls=%async_computation.1 | async-start | bytes 1048576 | tf_op jit(solution)/shard_map/all_to_all | solution.py:85
  51.8 125.2 %all-gather.3.cloned.1.call-start = ((), (), s32[]{:S(2)}) async-start(), calls=%async_computation.3 | async-start | bytes 2048000 | tf_op jit(solution)/shard_map/all_gather | solution.py:99
  83.8 4.1 copy-start.4
  83.8 4.5 copy-start.1
  87.5 2.8 slice-start
  88.3 2.1 slice-start.1
  93.1 2.2 copy-start
  95.3 53.4 %copy-start.8 = (s32[512]{0:T(512)S(1)}, s32[512]{0:T(512)}, u32[]{:S(2)}) copy-start(s32[512]{0:T(512)} %param.16) | copy-start | bytes 6148
  95.3 53.4 %copy-start.3 = (s32[128,1,4]{2,1,0:T(1,128)S(1)}, s32[128,1,4]{2,1,0:T(1,128)}, u32[]{:S(2)}) copy-start(s32[128,1,4]{2,1,0:T(1,128)} %copy-done.2) | copy-start | bytes 6148
Sparse Core Ops, SparseCore 0:
  148.1 28.8 all-gather.2
